TPU v7x, 128 devices: a whole 4x4x4 slice. The times are simulated.
128 devices in a mesh: dev: 128 (over x, y, z, core).
Axes of the slice: x: 4, y: 4, z: 4, core: 2. Of those that a mesh axis runs over, the one named last changes fastest.
Arguments:
- density: bfloat16 [1024, 262144], P('dev'), may hold values from -6 to 6
- flags: int32 [1024], P('dev'), may hold values 0 or 1
- courant: float32 [1024], P('dev'), may hold values from 0.1 to 0.9
- spectral: bfloat16 [1024, 1024], replicated, may hold values from -0.1875 to 0.1875
- tensor: bfloat16 [128, 1024, 1024], P('dev'), may hold values from -0.1875 to 0.1875
- owner: int32 [4], replicated, may hold values from 0 to 127, as said below
Outputs:
- coeffs: bfloat16 [1024, 262144], P(None, 'dev')
- collision: float32 [4, 262144], P(None, 'dev')
Inputs may be any that keep to these rules, and one draw needn't show every extreme that they name: `owner`: distinct slice indices, one of which is 127.
All inputs are finite; a program needn't handle non-finite values. No bound on the sum of `flags` on one device may be relied on, other than what follows from the above.
Results may differ from a plain program's by a relative error of at most 0.0064.
Values may be sent and summed in bfloat16 or wider, within the bound.
No kernel may reach another device: no remote copies, remote signals or barrier semaphores. Data moves between devices by JAX's collectives and lax.ppermute only.
A program may use at most 128 MiB of HBM per device.

v0:
```python
import functools
import math

import jax
import jax.numpy as jnp
from jax import lax
from jax.experimental import pallas as pl
from jax.experimental.pallas import tpu as pltpu
from jax.sharding import PartitionSpec as P

BLOCK = 256
LANES = 128
GROUP = 8
SUBLANES = 8
LIMIT = 24 << 20
HIGH = 58 << 20


def fold_kernel(t_hbm, u_ref, e_ref, t_ref, sems):
    count = t_ref.shape[0] // BLOCK
    halves = BLOCK // LANES
    copies = []
    for i in range(count):
        rows = pl.ds(i * BLOCK, BLOCK)
        copies.append(pltpu.make_async_copy(t_hbm.at[0, rows, :], t_ref.at[rows, :], sems.at[i]))
        copies[i].start()

    def load(i, j):
        return t_ref[pl.ds(i * BLOCK, BLOCK), pl.ds(j * BLOCK, BLOCK)].astype(jnp.float32)

    def store(at, block):
        block = block.astype(jnp.bfloat16)
        for half in range(halves):
            quarter, run = divmod(at * halves + half, 4)
            lines = block[:, half * LANES : (half + 1) * LANES].reshape(run_length, SUBLANES, LANES)
            u_ref[pl.ds(run * run_length, run_length), pl.ds(quarter * SUBLANES, SUBLANES), :] = lines

    run_length = BLOCK // SUBLANES
    row = lax.broadcasted_iota(jnp.int32, (BLOCK, BLOCK), 0)
    col = lax.broadcasted_iota(jnp.int32, (BLOCK, BLOCK), 1)
    above = above_pairs(count)
    e_ref[...] = jnp.zeros_like(e_ref)
    for j in range(count):
        copies[j].wait()
        for i in range(j):
            store(above.index((i, j)), load(i, j) + load(j, i).T)
        if j % 2 == 1:
            upper, lower = load(j - 1, j - 1), load(j, j)
            packed = jnp.where(row < col, upper + upper.T, jnp.where(row == col, upper, lower + lower.T))
            store(len(above) + j // 2, packed)
            line = jnp.sum(jnp.where(row == col, lower, 0.0), axis=0, keepdims=True).astype(jnp.bfloat16)
            for half in range(halves):
                e_ref[pl.ds(j // 2 * halves + half, 1), :] = line[:, half * LANES : (half + 1) * LANES]


def above_pairs(count):
    return [(i, j) for j in range(count) for i in range(j)]


def fold(tensor):
    size = tensor.shape[1]
    count = size // BLOCK
    rows = (len(above_pairs(count)) + count // 2) * BLOCK * (BLOCK // LANES)
    parts = rows // (4 * SUBLANES)
    return pl.pallas_call(
        fold_kernel,
        out_shape=[
            jax.ShapeDtypeStruct((parts, 4 * SUBLANES, LANES), jnp.bfloat16),
            jax.ShapeDtypeStruct((SUBLANES, LANES), jnp.bfloat16),
        ],
        in_specs=[pl.BlockSpec(memory_space=pltpu.HBM)],
        out_specs=[pl.BlockSpec(memory_space=pltpu.VMEM)] * 2,
        scratch_shapes=[pltpu.VMEM((size, size), jnp.bfloat16), pltpu.SemaphoreType.DMA((count,))],
        compiler_params=pltpu.CompilerParams(vmem_limit_bytes=HIGH),
        cost_estimate=pl.CostEstimate(flops=2 * size * size, bytes_accessed=3 * size * size, transcendentals=0),
        name="fold",
    )(tensor)


def advect_kernel(flags_ref, courant_ref, before_ref, here_ref, after_ref, out_ref):
    nodes = here_ref.shape[0]
    width = here_ref.shape[1] // out_ref.shape[0]
    row = lax.broadcasted_iota(jnp.int32, (nodes, 1), 0)
    flag = jnp.zeros((nodes, 1), jnp.int32)
    rate = jnp.zeros((nodes, 1), jnp.float32)
    for r in range(nodes):
        flag = jnp.where(row == r, flags_ref[r], flag)
        rate = jnp.where(row == r, courant_ref[r], rate)
    upward = jnp.broadcast_to(flag, (nodes, width)) == 1
    for d in range(out_ref.shape[0]):
        start, stop = d * width, (d + 1) * width
        last = d == out_ref.shape[0] - 1
        before = before_ref[...] if d == 0 else here_ref[:, start - LANES : start]
        after = after_ref[...] if last else here_ref[:, stop : stop + LANES]
        field = here_ref[:, start:stop].astype(jnp.float32)
        line = jnp.concatenate([before.astype(jnp.float32), field, after.astype(jnp.float32)], axis=1)
        left = pltpu.roll(line, 1, axis=1)[:, LANES : LANES + width]
        right = pltpu.roll(line, width + 2 * LANES - 1, axis=1)[:, LANES : LANES + width]
        neighbour = jnp.where(upward, left, right)
        moved = (field - rate * (field - neighbour)).astype(jnp.bfloat16)
        for t in range(width // LANES):
            out_ref[d, t * nodes : (t + 1) * nodes, :] = moved[:, t * LANES : (t + 1) * LANES]


def advect(density, flags, courant, parts, spare):
    nodes, cells = density.shape
    width = cells // parts
    wide = GROUP * width // LANES
    lines = cells // LANES
    rows = nodes * width // LANES
    return pl.pallas_call(
        advect_kernel,
        grid=(parts // GROUP,),
        out_shape=jax.ShapeDtypeStruct((parts, rows + spare, LANES), jnp.bfloat16),
        in_specs=[
            pl.BlockSpec(memory_space=pltpu.SMEM),
            pl.BlockSpec(memory_space=pltpu.SMEM),
            pl.BlockSpec((nodes, LANES), lambda i: (0, (i * wide + lines - 1) % lines)),
            pl.BlockSpec((nodes, GROUP * width), lambda i: (0, i)),
            pl.BlockSpec((nodes, LANES), lambda i: (0, ((i + 1) * wide) % lines)),
        ],
        out_specs=pl.BlockSpec((GROUP, rows, LANES), lambda i: (i, 0, 0)),
        compiler_params=pltpu.CompilerParams(vmem_limit_bytes=HIGH),
        cost_estimate=pl.CostEstimate(flops=4 * nodes * cells, bytes_accessed=4 * nodes * cells, transcendentals=0),
        name="advect",
    )(flags, courant, density, density, density)


def pick_kernel(owner_ref, pieces_hbm, extra_ref, _, out_hbm, chosen_ref, spread_ref, in_sems, sems):
    half = owner_ref.shape[0] // 2
    batch, rows = spread_ref.shape[0], spread_ref.shape[1]
    first = out_hbm.shape[1] - rows
    reads = []
    for m in range(2 * half):
        reads.append(pltpu.make_async_copy(pieces_hbm.at[owner_ref[m]], chosen_ref.at[m], in_sems.at[m]))
        reads[m].start()
    for read in reads:
        read.wait()
    extra = extra_ref[...]
    for d in range(batch):
        core, z, y = d % 2, d // 2 % 4, d // 8 % 4
        quarter = (y if core else z) * SUBLANES
        for s in range(half):
            part = chosen_ref[core * half + s, quarter : quarter + SUBLANES, :]
            spread_ref[d, s * SUBLANES : (s + 1) * SUBLANES, :] = part
        spread_ref[d, half * SUBLANES : (half + 1) * SUBLANES, :] = extra
    writes = []
    for b in range(out_hbm.shape[0] // batch):
        target = out_hbm.at[pl.ds(b * batch, batch), pl.ds(first, rows), :]
        writes.append(pltpu.make_async_copy(spread_ref, target, sems.at[b]))
    for write in writes:
        write.start()
    for write in writes:
        write.wait()


def pick(owner, pieces, extra, moved, spare, batch=32):
    parts = pieces.shape[0]
    return pl.pallas_call(
        pick_kernel,
        out_shape=jax.ShapeDtypeStruct(moved.shape, moved.dtype),
        in_specs=[
            pl.BlockSpec(memory_space=pltpu.SMEM),
            pl.BlockSpec(memory_space=pl.ANY),
            pl.BlockSpec(memory_space=pltpu.VMEM),
            pl.BlockSpec(memory_space=pl.ANY),
        ],
        out_specs=pl.BlockSpec(memory_space=pl.ANY),
        scratch_shapes=[
            pltpu.VMEM((owner.shape[0], *pieces.shape[1:]), jnp.bfloat16),
            pltpu.VMEM((batch, spare, LANES), jnp.bfloat16),
            pltpu.SemaphoreType.DMA((owner.shape[0],)),
            pltpu.SemaphoreType.DMA((parts // batch,)),
        ],
        input_output_aliases={3: 0},
        compiler_params=pltpu.CompilerParams(vmem_limit_bytes=HIGH),
        cost_estimate=pl.CostEstimate(flops=0, bytes_accessed=parts * spare * LANES * 2, transcendentals=0),
        name="pick",
    )(owner, pieces, extra, moved)


def unpack_kernel(owner_ref, arrived, near_ref, e_ref):
    end = arrived.shape[1] - SUBLANES
    near_ref[...] = arrived[:, end - near_ref.shape[1] : end, :]
    for m in range(e_ref.shape[0]):
        e_ref[m] = arrived[owner_ref[m], end:, :]


def unpack(owner, arrived, rows):
    slots = owner.shape[0]
    parts = arrived.shape[0]
    return pl.pallas_call(
        unpack_kernel,
        out_shape=[
            jax.ShapeDtypeStruct((parts, rows, LANES), jnp.bfloat16),
            jax.ShapeDtypeStruct((slots, SUBLANES, LANES), jnp.bfloat16),
        ],
        in_specs=[pl.BlockSpec(memory_space=pltpu.SMEM), pl.BlockSpec(memory_space=pltpu.VMEM)],
        out_specs=[pl.BlockSpec(memory_space=pltpu.VMEM)] * 2,
        compiler_params=pltpu.CompilerParams(vmem_limit_bytes=LIMIT),
        cost_estimate=pl.CostEstimate(flops=0, bytes_accessed=4 * parts * rows * LANES, transcendentals=0),
        name="unpack",
    )(owner, arrived)


def transform_kernel(tile, s_ref, x_ref, c_hbm, c_ref, sems):
    parts = x_ref.shape[0]
    nodes = s_ref.shape[1] // parts
    writes = []
    for n in range(c_ref.shape[1] // tile):
        lines = range(n * tile // LANES * nodes, (n + 1) * tile // LANES * nodes, nodes)
        columns = [x_ref[:, t : t + nodes, :].reshape(parts * nodes, LANES) for t in lines]
        block = jnp.concatenate(columns, axis=1)
        cells = pl.ds(n * tile, tile)
        c_ref[:, cells] = jnp.dot(s_ref[...], block, preferred_element_type=jnp.float32).astype(jnp.bfloat16)
        writes.append(pltpu.make_async_copy(c_ref.at[:, cells], c_hbm.at[:, cells], sems.at[n]))
        writes[n].start()
    for write in writes:
        write.wait()


def transform(spectral, arrived, width, tile=512):
    size = spectral.shape[0]
    return pl.pallas_call(
        functools.partial(transform_kernel, tile),
        out_shape=[jax.ShapeDtypeStruct((size, width), jnp.bfloat16)] * 2,
        in_specs=[pl.BlockSpec(memory_space=pltpu.VMEM)] * 2,
        out_specs=[pl.BlockSpec(memory_space=pl.ANY), pl.BlockSpec(memory_space=pltpu.VMEM)],
        scratch_shapes=[pltpu.SemaphoreType.DMA((width // tile,))],
        compiler_params=pltpu.CompilerParams(vmem_limit_bytes=LIMIT),
        cost_estimate=pl.CostEstimate(
            flops=2 * size * size * width, bytes_accessed=6 * size * width, transcendentals=0
        ),
        name="transform",
    )(spectral, arrived)


def quadratic_kernel(pairs, tile, e_ref, c_ref, *refs):
    sources, (out_ref, left_ref, item_ref) = refs[: len(pairs)], refs[-3:]
    size, width = c_ref.shape
    halves = BLOCK // LANES
    run = BLOCK // SUBLANES
    half = e_ref.shape[0] // 2
    above = above_pairs(size // BLOCK)
    row = lax.broadcasted_iota(jnp.int32, (BLOCK, BLOCK), 0)
    col = lax.broadcasted_iota(jnp.int32, (BLOCK, BLOCK), 1)
    factor = 1.0 / math.sqrt(size)
    here = lax.axis_index("dev")
    if len(refs) > len(pairs) + 3:
        out_ref[...] = refs[len(pairs)][...]
    else:
        out_ref[...] = jnp.zeros_like(out_ref)

    def put(at, both, i, j, place):
        left_ref[at] = jnp.concatenate(both, axis=0)
        for side, value in enumerate((i, j, place)):
            item_ref[side, at] = value

    items = jnp.int32(0)
    for source, (mine, k) in zip(sources, pairs):
        core = here % 2 if mine else 1 - here % 2
        quarter = (jnp.where(core == 0, here // 2, here // 8) + 4 - k) % 4
        place = core * half
        full = len(above) // 2

        def block(s, b, source=source):
            panels = []
            for part in range(halves):
                first = (b * halves + part) * run
                lines = source[first : first + run, s * SUBLANES : (s + 1) * SUBLANES, :]
                panels.append(lines.reshape(BLOCK, LANES))
            return jnp.concatenate(panels, axis=1)

        def choose(table, quarter=quarter):
            value = table[0]
            for at in range(1, len(table)):
                value = jnp.where(quarter == at, table[at], value)
            return value

        @pl.when(quarter < full)
        def _(block=block, choose=choose, place=place, items=items):
            for b in range(2):
                i, j = (choose([above[2 * q + b][side] for q in range(full)]) for side in range(2))
                put(items + b, [block(s, b) for s in range(half)], i, j, place)

        @pl.when(quarter == full)
        def _(block=block, place=place, items=items):
            for b in range(2):
                packed = [block(s, b).astype(jnp.float32) for s in range(half)]
                upper = [jnp.where(row <= col, x, 0.0).astype(jnp.bfloat16) for x in packed]
                lower = []
                for s, x in enumerate(packed):
                    values = [e_ref[place + s, pl.ds(b * halves + part, 1), :] for part in range(halves)]
                    line = jnp.concatenate(values, axis=1).astype(jnp.float32)
                    whole = jnp.where(row > col, x, jnp.where(row == col, line, 0.0))
                    lower.append(whole.astype(jnp.bfloat16))
                put(items + 2 * b, upper, 2 * b, 2 * b, place)
                put(items + 2 * b + 1, lower, 2 * b + 1, 2 * b + 1, place)

        items = items + jnp.where(quarter == full, 4, 2)

    def add(at):
        i, j, place = (item_ref[side, at] for side in range(3))
        left = pl.ds(pl.multiple_of(i * BLOCK, BLOCK), BLOCK)
        right = pl.ds(pl.multiple_of(j * BLOCK, BLOCK), BLOCK)
        for first in range(0, width, tile):
            cells = slice(first, first + tile)
            image = jnp.dot(left_ref[at], c_ref[right, cells], preferred_element_type=jnp.float32)
            weight = c_ref[left, cells].astype(jnp.float32)
            for s in range(half):
                term = image[s * BLOCK : (s + 1) * BLOCK] * weight
                line = jnp.sum(jnp.sum(term.reshape(run, SUBLANES, tile), axis=0), axis=0, keepdims=True)
                out_ref[pl.ds(place + s, 1), cells] += line * factor

    @pl.loop(0, items // 2)
    def _(at):
        add(2 * at)
        add(2 * at + 1)


def quadratic(pairs, sources, diagonals, coeffs, before=None, tile=512):
    size, width = coeffs.shape
    slots = diagonals.shape[0]
    args = [diagonals, coeffs, *sources] + ([] if before is None else [before])
    return pl.pallas_call(
        functools.partial(quadratic_kernel, pairs, tile),
        out_shape=jax.ShapeDtypeStruct((slots, width), jnp.float32),
        in_specs=[pl.BlockSpec(memory_space=pltpu.VMEM)] * len(args),
        out_specs=pl.BlockSpec(memory_space=pltpu.VMEM),
        scratch_shapes=[
            pltpu.VMEM((2 * len(pairs) + 4, slots // 2 * BLOCK, BLOCK), jnp.bfloat16),
            pltpu.SMEM((3, 2 * len(pairs) + 4), jnp.int32),
        ],
        compiler_params=pltpu.CompilerParams(vmem_limit_bytes=LIMIT),
        cost_estimate=pl.CostEstimate(
            flops=len(pairs) * size * size * width * 5 // 16, bytes_accessed=2 * size * width, transcendentals=0
        ),
        name="quadratic",
    )(*args)


def exchange(x):
    return lax.all_to_all(x, "dev", split_axis=0, concat_axis=0, tiled=True)


def shift(parts, k):
    pairs = []
    for d in range(parts):
        step = 8 if d % 2 else 2
        at = d // step % 4
        pairs.append((d, d + ((at + k) % 4 - at) * step))
    return pairs


def local(parts, density, flags, courant, spectral, tensor, owner):
    half = owner.shape[0] // 2
    width = density.shape[1] // parts
    spare = (half + 1) * SUBLANES
    folded, extra = fold(tensor)
    pieces = exchange(folded)
    moved = advect(density, flags, courant, parts, spare)
    arrived = exchange(pick(owner, pieces, extra, moved, spare))
    first, diagonals = unpack(owner, arrived, half * SUBLANES)
    pair = [(d, d ^ 1) for d in range(parts)]
    hops = (1, 2, 3)
    near = [lax.ppermute(first, "dev", shift(parts, k)) for k in hops]
    other = lax.ppermute(first, "dev", pair)
    result, coeffs = transform(spectral, arrived, width)
    begun = quadratic([(True, 0), (False, 0)], [first, other], diagonals, coeffs)
    *near, begun = lax.optimization_barrier((*near, begun))
    far = [lax.ppermute(x, "dev", pair) for x in near]
    own = quadratic([(True, k) for k in hops], near, diagonals, coeffs, begun)
    return (result, quadratic([(False, k) for k in hops], far, diagonals, coeffs, own))


def solution(mesh):
    in_specs = (P("dev", None), P("dev"), P("dev"), P(), P("dev", None, None), P())
    out_specs = (P(None, "dev"), P(None, "dev"))

    def step(*args):
        return local(mesh.shape["dev"], *args)

    return jax.shard_map(step, mesh=mesh, in_specs=in_specs, out_specs=out_specs, check_vma=False)
```

profile of v0, /device:TPU:1, one launch (start us, length us, event | category | flops | bytes accessed | tf_op | source)
XLA Modules:
  0.0 135.4 jit_solution(969506230301993990)
XLA Ops:
  0.6 2.8 %fold.1 = (bf16[128,32,128]{2,1,0:T(8,128)(2,1)}, bf16[8,128]{1,0:T(8,128)(2,1)}) custom-call(bf16[1,1024,1024]{2,1,0:T(8,128)(2,1)} %t_hbm.1), custom_call_target="tpu_custom_call" | custom-call | flops 2097152 | bytes 3145728 | tf_op jit(solution)/shard_map/fold/pallas_call | solution.py:65
  3.4 11.5 %all-to-all-start = ((bf16[128,32,128]{2,1,0:T(8,128)(2,1)}), bf16[128,32,128]{2,1,0:T(8,128)(2,1)S(1)}, u32[]{:S(2)}, u32[]{:S(2)}) async-start(bf16[128,32,128]{2,1,0:T(8,128)(2,1)} %get-tuple-element.12), calls=%async_computation | async-start | bytes 2097152 | tf_op jit(solution)/shard_map/all_to_all | solution.py:343
  14.9 11.8 %advect.1._ = bf16[128,152,128]{2,1,0:T(8,128)(2,1)} custom-call(s32[8]{0:T(128)} %flags_ref.1, f32[8]{0:T(128)} %courant_ref.1, bf16[8,262144]{1,0:T(8,128)(2,1)} %after_ref.1, bf16[8,262144]{1,0:T(8,128)(2,1)} %after_ref.1, bf16[8,262144]{1,0:T(8,128)(2,1)} %after_ref.1), custom_call_target="tpu_custom_call" | custom-call | flops 8388608 | bytes 8388608 | tf_op jit(solution)/shard_map/advect/pallas_call | solution.py:111
  26.7 7.5 %all-to-all-done.pieces_hbm = bf16[128,32,128]{2,1,0:T(8,128)(2,1)S(1)} async-done(((bf16[128,32,128]{2,1,0:T(8,128)(2,1)}), bf16[128,32,128]{2,1,0:T(8,128)(2,1)S(1)}, u32[]{:S(2)}, u32[]{:S(2)}) %all-to-all-start) | async-done | bytes 1048608 | tf_op jit(solution)/shard_map/all_to_all | solution.py:343
  34.2 0.0 copy-start.2
  34.2 1.0 copy-done.2
  35.2 2.5 %pick.1 = bf16[128,152,128]{2,1,0:T(8,128)(2,1)} custom-call(s32[4]{0:T(128)} %owner_ref.3, bf16[128,32,128]{2,1,0:T(8,128)(2,1)} %copy-done.2, bf16[8,128]{1,0:T(8,128)(2,1)} %get-tuple-element.13.extra_ref, bf16[128,152,128]{2,1,0:T(8,128)(2,1)} %advect.1._), custom_call_target="tpu_custom_call", output_to_operand_aliasing={{}: (3, {})} | custom-call | bytes 786432 | tf_op jit(solution)/shard_map/pick/pallas_call | solution.py:159
  37.7 0.0 copy-start
  37.7 66.5 %all_to_all.10.x_ref.arrived = bf16[128,152,128]{2,1,0:T(8,128)(2,1)S(1)} all-to-all(bf16[128,152,128]{2,1,0:T(8,128)(2,1)} %pick.1), channel_id=1, replica_groups=mesh['dev'=128] {'dev'}, dimensions={0} | all-to-all | bytes 9961472 | tf_op jit(solution)/shard_map/all_to_all | solution.py:343
  104.2 0.0 copy-done
  104.2 0.0 copy-start.1
  104.2 0.6 unpack.1
  104.8 1.2 collective-permute-start.3
  106.0 0.3 collective-permute-start
  106.3 1.2 collective-permute-start.1
  107.5 1.2 collective-permute-start.2
  108.7 0.0 copy-done.1
  108.7 5.5 %transform.1 = (bf16[1024,2048]{1,0:T(8,128)(2,1)}, bf16[1024,2048]{1,0:T(8,128)(2,1)S(1)}) custom-call(bf16[1024,1024]{1,0:T(8,128)(2,1)S(1)} %copy-done.1, bf16[128,152,128]{2,1,0:T(8,128)(2,1)S(1)} %all_to_all.10.x_ref.arrived), custom_call_target="tpu_custom_call" | custom-call | flops 4294967296 | bytes 12582912 | tf_op jit(solution)/shard_map/transform/pallas_call | solution.py:224
  114.2 0.0 collective-permute-done.3.refs_1_
  114.2 2.8 %quadratic.3.refs_3_ = f32[4,2048]{1,0:T(4,128)S(1)} custom-call(bf16[4,8,128]{2,1,0:T(8,128)(2,1)S(1)} %get-tuple-element.15.e_ref, bf16[1024,2048]{1,0:T(8,128)(2,1)S(1)} %get-tuple-element.16.c_ref, bf16[128,16,128]{2,1,0:T(8,128)(2,1)S(1)} %get-tuple-element.17.refs_0_, bf16[128,16,128]{2,1,0:T(8,128)(2,1)S(1)} %collective-permute-done.3.refs_1_), custom_call_target="tpu_custom_call" | custom-call | flops 1342177280 | bytes 4194304 | tf_op jit(solution)/shard_map/quadratic/pallas_call | solution.py:325
  117.0 4.2 %collective-permute-done.refs_0_ = bf16[128,16,128]{2,1,0:T(8,128)(2,1)S(1)} collective-permute-done((bf16[128,16,128]{2,1,0:T(8,128)(2,1)S(1)}, bf16[128,16,128]{2,1,0:T(8,128)(2,1)S(1)}, u32[]{:S(2)}, u32[]{:S(2)}) %collective-permute-start) | collective-permute-done | bytes 524320 | tf_op jit(solution)/shard_map/ppermute | solution.py:366
  121.2 0.0 collective-permute-done.1.refs_1_
  121.2 0.6 collective-permute-done.2.refs_2_
  121.8 1.2 collective-permute-start.4
  123.0 0.0 collective-permute-start.5
  123.0 0.5 collective-permute-start.6
  123.5 5.6 %quadratic.4.refs_3_ = f32[4,2048]{1,0:T(4,128)S(1)} custom-call(bf16[4,8,128]{2,1,0:T(8,128)(2,1)S(1)} %get-tuple-element.15.e_ref, bf16[1024,2048]{1,0:T(8,128)(2,1)S(1)} %get-tuple-element.16.c_ref, bf16[128,16,128]{2,1,0:T(8,128)(2,1)S(1)} %collective-permute-done.refs_0_, bf16[128,16,128]{2,1,0:T(8,128)(2,1)S(1)} %collective-permute-done.1.refs_1_, ...), custom_call_target="tpu_custom_call" | custom-call | flops 2013265920 | bytes 4194304 | tf_op jit(solution)/shard_map/quadratic/pallas_call | solution.py:325
  129.1 0.0 collective-permute-done.4.refs_0_
  129.1 0.0 collective-permute-done.5.refs_1_
  129.2 0.0 collective-permute-done.6.refs_2_
  129.2 6.2 %quadratic.5 = f32[4,2048]{1,0:T(4,128)} custom-call(bf16[4,8,128]{2,1,0:T(8,128)(2,1)S(1)} %get-tuple-element.15.e_ref, bf16[1024,2048]{1,0:T(8,128)(2,1)S(1)} %get-tuple-element.16.c_ref, bf16[128,16,128]{2,1,0:T(8,128)(2,1)S(1)} %collective-permute-done.4.refs_0_, bf16[128,16,128]{2,1,0:T(8,128)(2,1)S(1)} %collective-permute-done.5.refs_1_, ...), custom_call_target="tpu_custom_call" | custom-call | flops 2013265920 | bytes 4194304 | tf_op jit(solution)/shard_map/quadratic/pallas_call | solution.py:325
Async XLA Ops:
  3.4 30.8 %all-to-all-start = ((bf16[128,32,128]{2,1,0:T(8,128)(2,1)}), bf16[128,32,128]{2,1,0:T(8,128)(2,1)S(1)}, u32[]{:S(2)}, u32[]{:S(2)}) async-start(bf16[128,32,128]{2,1,0:T(8,128)(2,1)} %get-tuple-element.12), calls=%async_computation | async-start | bytes 2097152 | tf_op jit(solution)/shard_map/all_to_all | solution.py:343
  34.2 1.0 copy-start.2
  37.7 66.5 %copy-start = (s32[4]{0:T(128)S(1)}, s32[4]{0:T(128)}, u32[]{:S(2)}) copy-start(s32[4]{0:T(128)} %owner_ref.3) | copy-start | bytes 52
  104.2 4.5 %copy-start.1 = (bf16[1024,1024]{1,0:T(8,128)(2,1)S(1)}, bf16[1024,1024]{1,0:T(8,128)(2,1)}, u32[]{:S(2)}) copy-start(bf16[1024,1024]{1,0:T(8,128)(2,1)} %s_ref.1) | copy-start | bytes 6291460
  104.8 9.4 %collective-permute-start.3 = (bf16[128,16,128]{2,1,0:T(8,128)(2,1)S(1)}, bf16[128,16,128]{2,1,0:T(8,128)(2,1)S(1)}, u32[]{:S(2)}, u32[]{:S(2)}) collective-permute-start(bf16[128,16,128]{2,1,0:T(8,128)(2,1)S(1)} %get-tuple-element.17.refs_0_), channel_id=1, source_target_pairs={{0,1},{1,0},{2,3},{3,2},{4,5},{5,4},{6,7},{7,6},{8,9},{9,8},{10,11... | collective-permute-start | bytes 1572872 | tf_op jit(solution)/shard_map/ppermute | solution.py:367
  106.0 15.2 %collective-permute-start = (bf16[128,16,128]{2,1,0:T(8,128)(2,1)S(1)}, bf16[128,16,128]{2,1,0:T(8,128)(2,1)S(1)}, u32[]{:S(2)}, u32[]{:S(2)}) collective-permute-start(bf16[128,16,128]{2,1,0:T(8,128)(2,1)S(1)} %get-tuple-element.17.refs_0_), channel_id=1, source_target_pairs={{0,2},{1,9},{2,4},{3,11},{4,6},{5,13},{6,0},{7,15},{8,10},{9,17},{... | collective-permute-start | bytes 1572872 | tf_op jit(solution)/shard_map/ppermute | solution.py:366
  106.3 14.9 %collective-permute-start.1 = (bf16[128,16,128]{2,1,0:T(8,128)(2,1)S(1)}, bf16[128,16,128]{2,1,0:T(8,128)(2,1)S(1)}, u32[]{:S(2)}, u32[]{:S(2)}) collective-permute-start(bf16[128,16,128]{2,1,0:T(8,128)(2,1)S(1)} %get-tuple-element.17.refs_0_), channel_id=1, source_target_pairs={{0,4},{1,17},{2,6},{3,19},{4,0},{5,21},{6,2},{7,23},{8,12},{9,25},... | collective-permute-start | bytes 1572872 | tf_op jit(solution)/shard_map/ppermute | solution.py:366
  107.5 14.3 %collective-permute-start.2 = (bf16[128,16,128]{2,1,0:T(8,128)(2,1)S(1)}, bf16[128,16,128]{2,1,0:T(8,128)(2,1)S(1)}, u32[]{:S(2)}, u32[]{:S(2)}) collective-permute-start(bf16[128,16,128]{2,1,0:T(8,128)(2,1)S(1)} %get-tuple-element.17.refs_0_), channel_id=1, source_target_pairs={{0,6},{1,25},{2,0},{3,27},{4,2},{5,29},{6,4},{7,31},{8,14},{9,1},{... | collective-permute-start | bytes 1572872 | tf_op jit(solution)/shard_map/ppermute | solution.py:366
  121.8 7.3 %collective-permute-start.4 = (bf16[128,16,128]{2,1,0:T(8,128)(2,1)S(1)}, bf16[128,16,128]{2,1,0:T(8,128)(2,1)S(1)}, u32[]{:S(2)}, u32[]{:S(2)}) collective-permute-start(bf16[128,16,128]{2,1,0:T(8,128)(2,1)S(1)} %collective-permute-done.refs_0_), channel_id=1, source_target_pairs={{0,1},{1,0},{2,3},{3,2},{4,5},{5,4},{6,7},{7,6},{8,9},{9,8},{10,11... | collective-permute-start | bytes 1572872 | tf_op jit(solution)/shard_map/ppermute | solution.py:371
  123.0 6.1 %collective-permute-start.5 = (bf16[128,16,128]{2,1,0:T(8,128)(2,1)S(1)}, bf16[128,16,128]{2,1,0:T(8,128)(2,1)S(1)}, u32[]{:S(2)}, u32[]{:S(2)}) collective-permute-start(bf16[128,16,128]{2,1,0:T(8,128)(2,1)S(1)} %collective-permute-done.1.refs_1_), channel_id=1, source_target_pairs={{0,1},{1,0},{2,3},{3,2},{4,5},{5,4},{6,7},{7,6},{8,9},{9,8},{10,11... | collective-permute-start | bytes 1572872 | tf_op jit(solution)/shard_map/ppermute | solution.py:371
  123.0 6.1 %collective-permute-start.6 = (bf16[128,16,128]{2,1,0:T(8,128)(2,1)S(1)}, bf16[128,16,128]{2,1,0:T(8,128)(2,1)S(1)}, u32[]{:S(2)}, u32[]{:S(2)}) collective-permute-start(bf16[128,16,128]{2,1,0:T(8,128)(2,1)S(1)} %collective-permute-done.2.refs_2_), channel_id=1, source_target_pairs={{0,1},{1,0},{2,3},{3,2},{4,5},{5,4},{6,7},{7,6},{8,9},{9,8},{10,11... | collective-permute-start | bytes 1572872 | tf_op jit(solution)/shard_map/ppermute | solution.py:371
where the time goes:
time: 136 us; the launch traced here: 135 us
  blocking collectives  66.5 us (49%)
  Pallas kernels  37.8 us (28%)
  starting transfers between devices  17.2 us (13%)
  waiting for transfers between devices  12.3 us (9%)
    all_to_all x1, blocking collectives, exchange(): return lax.all_to_all(x, 'dev', split_axis=0, concat_axis=0, tiled=True)  66.5 us
    pallas_call x3, Pallas kernels, quadratic(): pl.pallas_call(functools.partial(quadratic_kernel, pairs, tile), out_shap...  14.6 us
    pallas_call x1, Pallas kernels, advect(): pl.pallas_call(advect_kernel, grid=(parts // GROUP,), out_shape=jax.Shape...  11.8 us
    all_to_all x1, starting transfers between devices, exchange(): return lax.all_to_all(x, 'dev', split_axis=0, concat_axis=0, tiled=True)  11.5 us
    all_to_all x1, waiting for transfers between devices, exchange(): return lax.all_to_all(x, 'dev', split_axis=0, concat_axis=0, tiled=True)  7.49 us
    pallas_call x1, Pallas kernels, transform(): pl.pallas_call(functools.partial(transform_kernel, tile), out_shape=[jax....  5.5 us
    ppermute x3, waiting for transfers between devices, local(): near = [lax.ppermute(first, 'dev', shift(parts, k)) for k in hops]  4.8 us
    pallas_call x1, Pallas kernels, fold(): pl.pallas_call(fold_kernel, out_shape=[jax.ShapeDtypeStruct((parts, 4 * S...  2.79 us
  transfers between devices with their start and end apart: 8, of which 3 were waited for; matrix products, arithmetic and copies ran while one was open for 0% of the time, Pallas kernels for 19%

commit v1 on v0

--- a/solution.py
+++ b/solution.py
@@ -13,7 +13,7 @@
 GROUP = 8
 SUBLANES = 8
 LIMIT = 24 << 20
-HIGH = 58 << 20
+HIGH = 63 << 20
 
 
 def fold_kernel(t_hbm, u_ref, e_ref, t_ref, sems):
@@ -126,22 +126,17 @@
     )(flags, courant, density, density, density)
 
 
-def pick_kernel(owner_ref, pieces_hbm, extra_ref, _, out_hbm, chosen_ref, spread_ref, in_sems, sems):
+def pick_kernel(owner_ref, pieces_ref, extra_ref, _, out_hbm, spread_ref, sems):
     half = owner_ref.shape[0] // 2
     batch, rows = spread_ref.shape[0], spread_ref.shape[1]
     first = out_hbm.shape[1] - rows
-    reads = []
-    for m in range(2 * half):
-        reads.append(pltpu.make_async_copy(pieces_hbm.at[owner_ref[m]], chosen_ref.at[m], in_sems.at[m]))
-        reads[m].start()
-    for read in reads:
-        read.wait()
+    chosen = [pieces_ref[owner_ref[m]] for m in range(2 * half)]
     extra = extra_ref[...]
     for d in range(batch):
         core, z, y = d % 2, d // 2 % 4, d // 8 % 4
         quarter = (y if core else z) * SUBLANES
         for s in range(half):
-            part = chosen_ref[core * half + s, quarter : quarter + SUBLANES, :]
+            part = chosen[core * half + s][quarter : quarter + SUBLANES, :]
             spread_ref[d, s * SUBLANES : (s + 1) * SUBLANES, :] = part
         spread_ref[d, half * SUBLANES : (half + 1) * SUBLANES, :] = extra
     writes = []
@@ -161,15 +156,13 @@
         out_shape=jax.ShapeDtypeStruct(moved.shape, moved.dtype),
         in_specs=[
             pl.BlockSpec(memory_space=pltpu.SMEM),
-            pl.BlockSpec(memory_space=pl.ANY),
+            pl.BlockSpec(memory_space=pltpu.VMEM),
             pl.BlockSpec(memory_space=pltpu.VMEM),
             pl.BlockSpec(memory_space=pl.ANY),
         ],
         out_specs=pl.BlockSpec(memory_space=pl.ANY),
         scratch_shapes=[
-            pltpu.VMEM((owner.shape[0], *pieces.shape[1:]), jnp.bfloat16),
             pltpu.VMEM((batch, spare, LANES), jnp.bfloat16),
-            pltpu.SemaphoreType.DMA((owner.shape[0],)),
             pltpu.SemaphoreType.DMA((parts // batch,)),
         ],
         input_output_aliases={3: 0},
@@ -362,15 +355,15 @@
     arrived = exchange(pick(owner, pieces, extra, moved, spare))
     first, diagonals = unpack(owner, arrived, half * SUBLANES)
     pair = [(d, d ^ 1) for d in range(parts)]
-    hops = (1, 2, 3)
-    near = [lax.ppermute(first, "dev", shift(parts, k)) for k in hops]
+    near = {k: lax.ppermute(first, "dev", shift(parts, k)) for k in (2, 1, 3)}
     other = lax.ppermute(first, "dev", pair)
     result, coeffs = transform(spectral, arrived, width)
-    begun = quadratic([(True, 0), (False, 0)], [first, other], diagonals, coeffs)
-    *near, begun = lax.optimization_barrier((*near, begun))
-    far = [lax.ppermute(x, "dev", pair) for x in near]
-    own = quadratic([(True, k) for k in hops], near, diagonals, coeffs, begun)
-    return (result, quadratic([(False, k) for k in hops], far, diagonals, coeffs, own))
+    sums = quadratic([(True, 0), (False, 0), (True, 3)], [first, other, near[3]], diagonals, coeffs)
+    near[1], near[2], near[3], sums = lax.optimization_barrier((near[1], near[2], near[3], sums))
+    far = {k: lax.ppermute(near[k], "dev", pair) for k in (1, 2, 3)}
+    sums = quadratic([(True, 1), (True, 2)], [near[1], near[2]], diagonals, coeffs, sums)
+    rest = (1, 2, 3)
+    return (result, quadratic([(False, k) for k in rest], [far[k] for k in rest], diagonals, coeffs, sums))
 
 
 def solution(mesh):

time: 136 us -> 133 us (0.978)
  transfers between devices with their start and end apart: 8 -> 8, of which waited for: 3 -> 2; matrix products, arithmetic and copies ran while one was open for 0% -> 0% of each run, Pallas kernels for 19% -> 19%
where the time goes in v1:
time: 133 us
  blocking collectives  66.5 us (50%)
  Pallas kernels  37.5 us (28%)
  starting transfers between devices  17.1 us (13%)
  waiting for transfers between devices  11 us (8%)
    all_to_all x1, blocking collectives, exchange(): return lax.all_to_all(x, 'dev', split_axis=0, concat_axis=0, tiled=True)  66.5 us
    pallas_call x3, Pallas kernels, quadratic(): pl.pallas_call(functools.partial(quadratic_kernel, pairs, tile), out_shap...  14.6 us
    all_to_all x1, starting transfers between devices, exchange(): return lax.all_to_all(x, 'dev', split_axis=0, concat_axis=0, tiled=True)  12 us
    pallas_call x1, Pallas kernels, advect(): pl.pallas_call(advect_kernel, grid=(parts // GROUP,), out_shape=jax.Shape...  11.8 us
    all_to_all x1, waiting for transfers between devices, exchange(): return lax.all_to_all(x, 'dev', split_axis=0, concat_axis=0, tiled=True)  7.13 us
    pallas_call x1, Pallas kernels, transform(): pl.pallas_call(functools.partial(transform_kernel, tile), out_shape=[jax....  5.5 us
    ppermute x3, waiting for transfers between devices, local(): near = {k: lax.ppermute(first, 'dev', shift(parts, k)) for k in (2, 1, 3)}  3.88 us
    pallas_call x1, Pallas kernels, fold(): pl.pallas_call(fold_kernel, out_shape=[jax.ShapeDtypeStruct((parts, 4 * S...  2.79 us
  transfers between devices with their start and end apart: 8, of which 2 were waited for; matrix products, arithmetic and copies ran while one was open for 0% of the time, Pallas kernels for 19%

profile of v1, /device:TPU:1, one launch (start us, length us, event | category | flops | bytes accessed | tf_op | source)
XLA Modules:
  0.0 132.8 jit_solution(6848034091401263225)
XLA Ops:
  0.6 2.8 %fold.1 = (bf16[128,32,128]{2,1,0:T(8,128)(2,1)}, bf16[8,128]{1,0:T(8,128)(2,1)}) custom-call(bf16[1,1024,1024]{2,1,0:T(8,128)(2,1)} %t_hbm.1), custom_call_target="tpu_custom_call" | custom-call | flops 2097152 | bytes 3145728 | tf_op jit(solution)/shard_map/fold/pallas_call | solution.py:65
  3.4 12.0 %all-to-all-start = ((bf16[128,32,128]{2,1,0:T(8,128)(2,1)}), bf16[128,32,128]{2,1,0:T(8,128)(2,1)}, u32[]{:S(2)}, u32[]{:S(2)}) async-start(bf16[128,32,128]{2,1,0:T(8,128)(2,1)} %get-tuple-element.12), calls=%async_computation | async-start | bytes 2097152 | tf_op jit(solution)/shard_map/all_to_all | solution.py:336
  15.4 11.8 %advect.1._ = bf16[128,152,128]{2,1,0:T(8,128)(2,1)} custom-call(s32[8]{0:T(128)} %flags_ref.1, f32[8]{0:T(128)} %courant_ref.1, bf16[8,262144]{1,0:T(8,128)(2,1)} %after_ref.1, bf16[8,262144]{1,0:T(8,128)(2,1)} %after_ref.1, bf16[8,262144]{1,0:T(8,128)(2,1)} %after_ref.1), custom_call_target="tpu_custom_call" | custom-call | flops 8388608 | bytes 8388608 | tf_op jit(solution)/shard_map/advect/pallas_call | solution.py:111
  27.2 7.1 %all-to-all-done.pieces_ref = bf16[128,32,128]{2,1,0:T(8,128)(2,1)} async-done(((bf16[128,32,128]{2,1,0:T(8,128)(2,1)}), bf16[128,32,128]{2,1,0:T(8,128)(2,1)}, u32[]{:S(2)}, u32[]{:S(2)}) %all-to-all-start) | async-done | bytes 1048608 | tf_op jit(solution)/shard_map/all_to_all | solution.py:336
  34.3 2.2 %pick.1 = bf16[128,152,128]{2,1,0:T(8,128)(2,1)} custom-call(s32[4]{0:T(128)} %owner_ref.3, bf16[128,32,128]{2,1,0:T(8,128)(2,1)} %all-to-all-done.pieces_ref, bf16[8,128]{1,0:T(8,128)(2,1)} %get-tuple-element.13.extra_ref, bf16[128,152,128]{2,1,0:T(8,128)(2,1)} %advect.1._), custom_call_target="tpu_custom_call", output_to_operand_aliasing={{}: (3, {})} | custom-call | bytes 786432 | tf_op jit(solution)/shard_map/pick/pallas_call | solution.py:154
  36.6 0.0 copy-start
  36.6 66.5 %all_to_all.10.x_ref.arrived = bf16[128,152,128]{2,1,0:T(8,128)(2,1)S(1)} all-to-all(bf16[128,152,128]{2,1,0:T(8,128)(2,1)} %pick.1), channel_id=1, replica_groups=mesh['dev'=128] {'dev'}, dimensions={0} | all-to-all | bytes 9961472 | tf_op jit(solution)/shard_map/all_to_all | solution.py:336
  103.0 0.0 copy-done
  103.0 0.0 copy-start.1
  103.0 0.6 unpack.1
  103.6 1.0 collective-permute-start.2
  104.6 1.1 collective-permute-start.3
  105.8 0.0 collective-permute-start
  105.8 1.6 %collective-permute-start.1 = (bf16[128,16,128]{2,1,0:T(8,128)(2,1)S(1)}, bf16[128,16,128]{2,1,0:T(8,128)(2,1)S(1)}, u32[]{:S(2)}, u32[]{:S(2)}) collective-permute-start(bf16[128,16,128]{2,1,0:T(8,128)(2,1)S(1)} %get-tuple-element.17.refs_0_), channel_id=1, source_target_pairs={{0,4},{1,17},{2,6},{3,19},{4,0},{5,21},{6,2},{7,23},{8,12},{9,25},... | collective-permute-start | bytes 1572872 | tf_op jit(solution)/shard_map/ppermute | solution.py:358
  107.4 0.0 copy-done.1
  107.4 5.5 %transform.1 = (bf16[1024,2048]{1,0:T(8,128)(2,1)}, bf16[1024,2048]{1,0:T(8,128)(2,1)S(1)}) custom-call(bf16[1024,1024]{1,0:T(8,128)(2,1)S(1)} %copy-done.1, bf16[128,152,128]{2,1,0:T(8,128)(2,1)S(1)} %all_to_all.10.x_ref.arrived), custom_call_target="tpu_custom_call" | custom-call | flops 4294967296 | bytes 12582912 | tf_op jit(solution)/shard_map/transform/pallas_call | solution.py:217
  112.9 0.0 collective-permute-done.2.refs_2_
  112.9 0.0 collective-permute-done.3.refs_1_
  112.9 4.1 %quadratic.3.refs_2_ = f32[4,2048]{1,0:T(4,128)S(1)} custom-call(bf16[4,8,128]{2,1,0:T(8,128)(2,1)S(1)} %get-tuple-element.15.e_ref, bf16[1024,2048]{1,0:T(8,128)(2,1)S(1)} %get-tuple-element.16.c_ref, bf16[128,16,128]{2,1,0:T(8,128)(2,1)S(1)} %get-tuple-element.17.refs_0_, bf16[128,16,128]{2,1,0:T(8,128)(2,1)S(1)} %collective-permute-done.3.refs_1_, ...), custom_call_target="tpu_custom_call" | custom-call | flops 2013265920 | bytes 4194304 | tf_op jit(solution)/shard_map/quadratic/pallas_call | solution.py:318
  117.0 3.9 %collective-permute-done.refs_0_ = bf16[128,16,128]{2,1,0:T(8,128)(2,1)S(1)} collective-permute-done((bf16[128,16,128]{2,1,0:T(8,128)(2,1)S(1)}, bf16[128,16,128]{2,1,0:T(8,128)(2,1)S(1)}, u32[]{:S(2)}, u32[]{:S(2)}) %collective-permute-start) | collective-permute-done | bytes 524320 | tf_op jit(solution)/shard_map/ppermute | solution.py:358
  120.9 0.0 collective-permute-done.1.refs_1_
  120.9 0.9 collective-permute-start.4
  121.8 0.0 collective-permute-start.5
  121.8 0.5 collective-permute-start.6
  122.3 4.2 %quadratic.4.refs_3_ = f32[4,2048]{1,0:T(4,128)S(1)} custom-call(bf16[4,8,128]{2,1,0:T(8,128)(2,1)S(1)} %get-tuple-element.15.e_ref, bf16[1024,2048]{1,0:T(8,128)(2,1)S(1)} %get-tuple-element.16.c_ref, bf16[128,16,128]{2,1,0:T(8,128)(2,1)S(1)} %collective-permute-done.refs_0_, bf16[128,16,128]{2,1,0:T(8,128)(2,1)S(1)} %collective-permute-done.1.refs_1_, ...), custom_call_target="tpu_custom_call" | custom-call | flops 1342177280 | bytes 4194304 | tf_op jit(solution)/shard_map/quadratic/pallas_call | solution.py:318
  126.5 0.0 collective-permute-done.4.refs_0_
  126.5 0.0 collective-permute-done.5.refs_1_
  126.5 0.0 collective-permute-done.6.refs_2_
  126.5 6.2 %quadratic.5 = f32[4,2048]{1,0:T(4,128)} custom-call(bf16[4,8,128]{2,1,0:T(8,128)(2,1)S(1)} %get-tuple-element.15.e_ref, bf16[1024,2048]{1,0:T(8,128)(2,1)S(1)} %get-tuple-element.16.c_ref, bf16[128,16,128]{2,1,0:T(8,128)(2,1)S(1)} %collective-permute-done.4.refs_0_, bf16[128,16,128]{2,1,0:T(8,128)(2,1)S(1)} %collective-permute-done.5.refs_1_, ...), custom_call_target="tpu_custom_call" | custom-call | flops 2013265920 | bytes 4194304 | tf_op jit(solution)/shard_map/quadratic/pallas_call | solution.py:318
Async XLA Ops:
  3.4 30.9 %all-to-all-start = ((bf16[128,32,128]{2,1,0:T(8,128)(2,1)}), bf16[128,32,128]{2,1,0:T(8,128)(2,1)}, u32[]{:S(2)}, u32[]{:S(2)}) async-start(bf16[128,32,128]{2,1,0:T(8,128)(2,1)} %get-tuple-element.12), calls=%async_computation | async-start | bytes 2097152 | tf_op jit(solution)/shard_map/all_to_all | solution.py:336
  36.6 66.5 %copy-start = (s32[4]{0:T(128)S(1)}, s32[4]{0:T(128)}, u32[]{:S(2)}) copy-start(s32[4]{0:T(128)} %owner_ref.3) | copy-start | bytes 52
  103.0 4.3 %copy-start.1 = (bf16[1024,1024]{1,0:T(8,128)(2,1)S(1)}, bf16[1024,1024]{1,0:T(8,128)(2,1)}, u32[]{:S(2)}) copy-start(bf16[1024,1024]{1,0:T(8,128)(2,1)} %s_ref.1) | copy-start | bytes 6291460
  103.6 9.2 %collective-permute-start.2 = (bf16[128,16,128]{2,1,0:T(8,128)(2,1)S(1)}, bf16[128,16,128]{2,1,0:T(8,128)(2,1)S(1)}, u32[]{:S(2)}, u32[]{:S(2)}) collective-permute-start(bf16[128,16,128]{2,1,0:T(8,128)(2,1)S(1)} %get-tuple-element.17.refs_0_), channel_id=1, source_target_pairs={{0,6},{1,25},{2,0},{3,27},{4,2},{5,29},{6,4},{7,31},{8,14},{9,1},{... | collective-permute-start | bytes 1572872 | tf_op jit(solution)/shard_map/ppermute | solution.py:358
  104.6 8.3 %collective-permute-start.3 = (bf16[128,16,128]{2,1,0:T(8,128)(2,1)S(1)}, bf16[128,16,128]{2,1,0:T(8,128)(2,1)S(1)}, u32[]{:S(2)}, u32[]{:S(2)}) collective-permute-start(bf16[128,16,128]{2,1,0:T(8,128)(2,1)S(1)} %get-tuple-element.17.refs_0_), channel_id=1, source_target_pairs={{0,1},{1,0},{2,3},{3,2},{4,5},{5,4},{6,7},{7,6},{8,9},{9,8},{10,11... | collective-permute-start | bytes 1572872 | tf_op jit(solution)/shard_map/ppermute | solution.py:359
  105.8 15.2 %collective-permute-start = (bf16[128,16,128]{2,1,0:T(8,128)(2,1)S(1)}, bf16[128,16,128]{2,1,0:T(8,128)(2,1)S(1)}, u32[]{:S(2)}, u32[]{:S(2)}) collective-permute-start(bf16[128,16,128]{2,1,0:T(8,128)(2,1)S(1)} %get-tuple-element.17.refs_0_), channel_id=1, source_target_pairs={{0,2},{1,9},{2,4},{3,11},{4,6},{5,13},{6,0},{7,15},{8,10},{9,17},{... | collective-permute-start | bytes 1572872 | tf_op jit(solution)/shard_map/ppermute | solution.py:358
  105.8 15.2 %collective-permute-start.1 = (bf16[128,16,128]{2,1,0:T(8,128)(2,1)S(1)}, bf16[128,16,128]{2,1,0:T(8,128)(2,1)S(1)}, u32[]{:S(2)}, u32[]{:S(2)}) collective-permute-start(bf16[128,16,128]{2,1,0:T(8,128)(2,1)S(1)} %get-tuple-element.17.refs_0_), channel_id=1, source_target_pairs={{0,4},{1,17},{2,6},{3,19},{4,0},{5,21},{6,2},{7,23},{8,12},{9,25},... | collective-permute-start | bytes 1572872 | tf_op jit(solution)/shard_map/ppermute | solution.py:358
  120.9 5.6 %collective-permute-start.4 = (bf16[128,16,128]{2,1,0:T(8,128)(2,1)S(1)}, bf16[128,16,128]{2,1,0:T(8,128)(2,1)S(1)}, u32[]{:S(2)}, u32[]{:S(2)}) collective-permute-start(bf16[128,16,128]{2,1,0:T(8,128)(2,1)S(1)} %collective-permute-done.refs_0_), channel_id=1, source_target_pairs={{0,1},{1,0},{2,3},{3,2},{4,5},{5,4},{6,7},{7,6},{8,9},{9,8},{10,11... | collective-permute-start | bytes 1572872 | tf_op jit(solution)/shard_map/ppermute | solution.py:363
  121.8 4.7 %collective-permute-start.5 = (bf16[128,16,128]{2,1,0:T(8,128)(2,1)S(1)}, bf16[128,16,128]{2,1,0:T(8,128)(2,1)S(1)}, u32[]{:S(2)}, u32[]{:S(2)}) collective-permute-start(bf16[128,16,128]{2,1,0:T(8,128)(2,1)S(1)} %collective-permute-done.1.refs_1_), channel_id=1, source_target_pairs={{0,1},{1,0},{2,3},{3,2},{4,5},{5,4},{6,7},{7,6},{8,9},{9,8},{10,11... | collective-permute-start | bytes 1572872 | tf_op jit(solution)/shard_map/ppermute | solution.py:363
  121.8 4.7 %collective-permute-start.6 = (bf16[128,16,128]{2,1,0:T(8,128)(2,1)S(1)}, bf16[128,16,128]{2,1,0:T(8,128)(2,1)S(1)}, u32[]{:S(2)}, u32[]{:S(2)}) collective-permute-start(bf16[128,16,128]{2,1,0:T(8,128)(2,1)S(1)} %collective-permute-done.2.refs_2_), channel_id=1, source_target_pairs={{0,1},{1,0},{2,3},{3,2},{4,5},{5,4},{6,7},{7,6},{8,9},{9,8},{10,11... | collective-permute-start | bytes 1572872 | tf_op jit(solution)/shard_map/ppermute | solution.py:363

commit v2 on v1

--- a/solution.py
+++ b/solution.py
@@ -305,10 +305,15 @@
                 line = jnp.sum(jnp.sum(term.reshape(run, SUBLANES, tile), axis=0), axis=0, keepdims=True)
                 out_ref[pl.ds(place + s, 1), cells] += line * factor
 
-    @pl.loop(0, items // 2)
+    @pl.loop(0, items // 4)
     def _(at):
-        add(2 * at)
-        add(2 * at + 1)
+        for step in range(4):
+            add(4 * at + step)
+
+    @pl.when(items % 4 == 2)
+    def _():
+        add(items - 2)
+        add(items - 1)
 
 
 def quadratic(pairs, sources, diagonals, coeffs, before=None, tile=512):

time: 133 us -> 133 us (level)
  no operation moved by 1% of the time
where the time goes in v2:
time: 133 us; the launch traced here: 132 us
  blocking collectives  66.5 us (50%)
  Pallas kernels  36.7 us (28%)
  starting transfers between devices  17.1 us (13%)
  waiting for transfers between devices  11.2 us (8%)
    all_to_all x1, blocking collectives, exchange(): return lax.all_to_all(x, 'dev', split_axis=0, concat_axis=0, tiled=True)  66.5 us
    pallas_call x3, Pallas kernels, quadratic(): pl.pallas_call(functools.partial(quadratic_kernel, pairs, tile), out_shap...  13.8 us
    all_to_all x1, starting transfers between devices, exchange(): return lax.all_to_all(x, 'dev', split_axis=0, concat_axis=0, tiled=True)  12 us
    pallas_call x1, Pallas kernels, advect(): pl.pallas_call(advect_kernel, grid=(parts // GROUP,), out_shape=jax.Shape...  11.8 us
    all_to_all x1, waiting for transfers between devices, exchange(): return lax.all_to_all(x, 'dev', split_axis=0, concat_axis=0, tiled=True)  7.13 us
    pallas_call x1, Pallas kernels, transform(): pl.pallas_call(functools.partial(transform_kernel, tile), out_shape=[jax....  5.5 us
    ppermute x3, waiting for transfers between devices, local(): near = {k: lax.ppermute(first, 'dev', shift(parts, k)) for k in (2, 1, 3)}  4.08 us
    pallas_call x1, Pallas kernels, fold(): pl.pallas_call(fold_kernel, out_shape=[jax.ShapeDtypeStruct((parts, 4 * S...  2.79 us
  transfers between devices with their start and end apart: 8, of which 2 were waited for; matrix products, arithmetic and copies ran while one was open for 0% of the time, Pallas kernels for 19%

profile of v2, /device:TPU:1, one launch (start us, length us, event | category | flops | bytes accessed | tf_op | source)
XLA Modules:
  0.0 132.2 jit_solution(1011553655976832550)
XLA Ops:
  0.6 2.8 %fold.1 = (bf16[128,32,128]{2,1,0:T(8,128)(2,1)}, bf16[8,128]{1,0:T(8,128)(2,1)}) custom-call(bf16[1,1024,1024]{2,1,0:T(8,128)(2,1)} %t_hbm.1), custom_call_target="tpu_custom_call" | custom-call | flops 2097152 | bytes 3145728 | tf_op jit(solution)/shard_map/fold/pallas_call | solution.py:65
  3.4 12.0 %all-to-all-start = ((bf16[128,32,128]{2,1,0:T(8,128)(2,1)}), bf16[128,32,128]{2,1,0:T(8,128)(2,1)}, u32[]{:S(2)}, u32[]{:S(2)}) async-start(bf16[128,32,128]{2,1,0:T(8,128)(2,1)} %get-tuple-element.12), calls=%async_computation | async-start | bytes 2097152 | tf_op jit(solution)/shard_map/all_to_all | solution.py:341
  15.4 11.8 %advect.1._ = bf16[128,152,128]{2,1,0:T(8,128)(2,1)} custom-call(s32[8]{0:T(128)} %flags_ref.1, f32[8]{0:T(128)} %courant_ref.1, bf16[8,262144]{1,0:T(8,128)(2,1)} %after_ref.1, bf16[8,262144]{1,0:T(8,128)(2,1)} %after_ref.1, bf16[8,262144]{1,0:T(8,128)(2,1)} %after_ref.1), custom_call_target="tpu_custom_call" | custom-call | flops 8388608 | bytes 8388608 | tf_op jit(solution)/shard_map/advect/pallas_call | solution.py:111
  27.2 7.1 %all-to-all-done.pieces_ref = bf16[128,32,128]{2,1,0:T(8,128)(2,1)} async-done(((bf16[128,32,128]{2,1,0:T(8,128)(2,1)}), bf16[128,32,128]{2,1,0:T(8,128)(2,1)}, u32[]{:S(2)}, u32[]{:S(2)}) %all-to-all-start) | async-done | bytes 1048608 | tf_op jit(solution)/shard_map/all_to_all | solution.py:341
  34.3 2.2 %pick.1 = bf16[128,152,128]{2,1,0:T(8,128)(2,1)} custom-call(s32[4]{0:T(128)} %owner_ref.3, bf16[128,32,128]{2,1,0:T(8,128)(2,1)} %all-to-all-done.pieces_ref, bf16[8,128]{1,0:T(8,128)(2,1)} %get-tuple-element.13.extra_ref, bf16[128,152,128]{2,1,0:T(8,128)(2,1)} %advect.1._), custom_call_target="tpu_custom_call", output_to_operand_aliasing={{}: (3, {})} | custom-call | bytes 786432 | tf_op jit(solution)/shard_map/pick/pallas_call | solution.py:154
  36.6 0.0 copy-start
  36.6 66.5 %all_to_all.10.x_ref.arrived = bf16[128,152,128]{2,1,0:T(8,128)(2,1)S(1)} all-to-all(bf16[128,152,128]{2,1,0:T(8,128)(2,1)} %pick.1), channel_id=1, replica_groups=mesh['dev'=128] {'dev'}, dimensions={0} | all-to-all | bytes 9961472 | tf_op jit(solution)/shard_map/all_to_all | solution.py:341
  103.0 0.0 copy-done
  103.0 0.0 copy-start.1
  103.0 0.6 unpack.1
  103.6 1.0 collective-permute-start.2
  104.6 1.1 collective-permute-start.3
  105.8 0.0 collective-permute-start
  105.8 1.6 %collective-permute-start.1 = (bf16[128,16,128]{2,1,0:T(8,128)(2,1)S(1)}, bf16[128,16,128]{2,1,0:T(8,128)(2,1)S(1)}, u32[]{:S(2)}, u32[]{:S(2)}) collective-permute-start(bf16[128,16,128]{2,1,0:T(8,128)(2,1)S(1)} %get-tuple-element.17.refs_0_), channel_id=1, source_target_pairs={{0,4},{1,17},{2,6},{3,19},{4,0},{5,21},{6,2},{7,23},{8,12},{9,25},... | collective-permute-start | bytes 1572872 | tf_op jit(solution)/shard_map/ppermute | solution.py:363
  107.4 0.0 copy-done.1
  107.4 5.5 %transform.1 = (bf16[1024,2048]{1,0:T(8,128)(2,1)}, bf16[1024,2048]{1,0:T(8,128)(2,1)S(1)}) custom-call(bf16[1024,1024]{1,0:T(8,128)(2,1)S(1)} %copy-done.1, bf16[128,152,128]{2,1,0:T(8,128)(2,1)S(1)} %all_to_all.10.x_ref.arrived), custom_call_target="tpu_custom_call" | custom-call | flops 4294967296 | bytes 12582912 | tf_op jit(solution)/shard_map/transform/pallas_call | solution.py:217
  112.9 0.0 collective-permute-done.2.refs_2_
  112.9 0.0 collective-permute-done.3.refs_1_
  112.9 4.0 %quadratic.3.refs_2_ = f32[4,2048]{1,0:T(4,128)S(1)} custom-call(bf16[4,8,128]{2,1,0:T(8,128)(2,1)S(1)} %get-tuple-element.15.e_ref, bf16[1024,2048]{1,0:T(8,128)(2,1)S(1)} %get-tuple-element.16.c_ref, bf16[128,16,128]{2,1,0:T(8,128)(2,1)S(1)} %get-tuple-element.17.refs_0_, bf16[128,16,128]{2,1,0:T(8,128)(2,1)S(1)} %collective-permute-done.3.refs_1_, ...), custom_call_target="tpu_custom_call" | custom-call | flops 2013265920 | bytes 4194304 | tf_op jit(solution)/shard_map/quadratic/pallas_call | solution.py:323
  116.8 4.1 %collective-permute-done.refs_0_ = bf16[128,16,128]{2,1,0:T(8,128)(2,1)S(1)} collective-permute-done((bf16[128,16,128]{2,1,0:T(8,128)(2,1)S(1)}, bf16[128,16,128]{2,1,0:T(8,128)(2,1)S(1)}, u32[]{:S(2)}, u32[]{:S(2)}) %collective-permute-start) | collective-permute-done | bytes 524320 | tf_op jit(solution)/shard_map/ppermute | solution.py:363
  120.9 0.0 collective-permute-done.1.refs_1_
  120.9 0.9 collective-permute-start.4
  121.8 0.0 collective-permute-start.5
  121.8 0.5 collective-permute-start.6
  122.3 4.0 %quadratic.4.refs_3_ = f32[4,2048]{1,0:T(4,128)S(1)} custom-call(bf16[4,8,128]{2,1,0:T(8,128)(2,1)S(1)} %get-tuple-element.15.e_ref, bf16[1024,2048]{1,0:T(8,128)(2,1)S(1)} %get-tuple-element.16.c_ref, bf16[128,16,128]{2,1,0:T(8,128)(2,1)S(1)} %collective-permute-done.refs_0_, bf16[128,16,128]{2,1,0:T(8,128)(2,1)S(1)} %collective-permute-done.1.refs_1_, ...), custom_call_target="tpu_custom_call" | custom-call | flops 1342177280 | bytes 4194304 | tf_op jit(solution)/shard_map/quadratic/pallas_call | solution.py:323
  126.3 0.0 collective-permute-done.4.refs_0_
  126.3 0.0 collective-permute-done.5.refs_1_
  126.3 0.0 collective-permute-done.6.refs_2_
  126.3 5.8 %quadratic.5 = f32[4,2048]{1,0:T(4,128)} custom-call(bf16[4,8,128]{2,1,0:T(8,128)(2,1)S(1)} %get-tuple-element.15.e_ref, bf16[1024,2048]{1,0:T(8,128)(2,1)S(1)} %get-tuple-element.16.c_ref, bf16[128,16,128]{2,1,0:T(8,128)(2,1)S(1)} %collective-permute-done.4.refs_0_, bf16[128,16,128]{2,1,0:T(8,128)(2,1)S(1)} %collective-permute-done.5.refs_1_, ...), custom_call_target="tpu_custom_call" | custom-call | flops 2013265920 | bytes 4194304 | tf_op jit(solution)/shard_map/quadratic/pallas_call | solution.py:323
Async XLA Ops:
  3.4 30.9 %all-to-all-start = ((bf16[128,32,128]{2,1,0:T(8,128)(2,1)}), bf16[128,32,128]{2,1,0:T(8,128)(2,1)}, u32[]{:S(2)}, u32[]{:S(2)}) async-start(bf16[128,32,128]{2,1,0:T(8,128)(2,1)} %get-tuple-element.12), calls=%async_computation | async-start | bytes 2097152 | tf_op jit(solution)/shard_map/all_to_all | solution.py:341
  36.6 66.5 %copy-start = (s32[4]{0:T(128)S(1)}, s32[4]{0:T(128)}, u32[]{:S(2)}) copy-start(s32[4]{0:T(128)} %owner_ref.3) | copy-start | bytes 52
  103.0 4.3 %copy-start.1 = (bf16[1024,1024]{1,0:T(8,128)(2,1)S(1)}, bf16[1024,1024]{1,0:T(8,128)(2,1)}, u32[]{:S(2)}) copy-start(bf16[1024,1024]{1,0:T(8,128)(2,1)} %s_ref.1) | copy-start | bytes 6291460
  103.6 9.2 %collective-permute-start.2 = (bf16[128,16,128]{2,1,0:T(8,128)(2,1)S(1)}, bf16[128,16,128]{2,1,0:T(8,128)(2,1)S(1)}, u32[]{:S(2)}, u32[]{:S(2)}) collective-permute-start(bf16[128,16,128]{2,1,0:T(8,128)(2,1)S(1)} %get-tuple-element.17.refs_0_), channel_id=1, source_target_pairs={{0,6},{1,25},{2,0},{3,27},{4,2},{5,29},{6,4},{7,31},{8,14},{9,1},{... | collective-permute-start | bytes 1572872 | tf_op jit(solution)/shard_map/ppermute | solution.py:363
  104.6 8.3 %collective-permute-start.3 = (bf16[128,16,128]{2,1,0:T(8,128)(2,1)S(1)}, bf16[128,16,128]{2,1,0:T(8,128)(2,1)S(1)}, u32[]{:S(2)}, u32[]{:S(2)}) collective-permute-start(bf16[128,16,128]{2,1,0:T(8,128)(2,1)S(1)} %get-tuple-element.17.refs_0_), channel_id=1, source_target_pairs={{0,1},{1,0},{2,3},{3,2},{4,5},{5,4},{6,7},{7,6},{8,9},{9,8},{10,11... | collective-permute-start | bytes 1572872 | tf_op jit(solution)/shard_map/ppermute | solution.py:364
  105.8 15.2 %collective-permute-start = (bf16[128,16,128]{2,1,0:T(8,128)(2,1)S(1)}, bf16[128,16,128]{2,1,0:T(8,128)(2,1)S(1)}, u32[]{:S(2)}, u32[]{:S(2)}) collective-permute-start(bf16[128,16,128]{2,1,0:T(8,128)(2,1)S(1)} %get-tuple-element.17.refs_0_), channel_id=1, source_target_pairs={{0,2},{1,9},{2,4},{3,11},{4,6},{5,13},{6,0},{7,15},{8,10},{9,17},{... | collective-permute-start | bytes 1572872 | tf_op jit(solution)/shard_map/ppermute | solution.py:363
  105.8 15.2 %collective-permute-start.1 = (bf16[128,16,128]{2,1,0:T(8,128)(2,1)S(1)}, bf16[128,16,128]{2,1,0:T(8,128)(2,1)S(1)}, u32[]{:S(2)}, u32[]{:S(2)}) collective-permute-start(bf16[128,16,128]{2,1,0:T(8,128)(2,1)S(1)} %get-tuple-element.17.refs_0_), channel_id=1, source_target_pairs={{0,4},{1,17},{2,6},{3,19},{4,0},{5,21},{6,2},{7,23},{8,12},{9,25},... | collective-permute-start | bytes 1572872 | tf_op jit(solution)/shard_map/ppermute | solution.py:363
  120.9 5.4 %collective-permute-start.4 = (bf16[128,16,128]{2,1,0:T(8,128)(2,1)S(1)}, bf16[128,16,128]{2,1,0:T(8,128)(2,1)S(1)}, u32[]{:S(2)}, u32[]{:S(2)}) collective-permute-start(bf16[128,16,128]{2,1,0:T(8,128)(2,1)S(1)} %collective-permute-done.refs_0_), channel_id=1, source_target_pairs={{0,1},{1,0},{2,3},{3,2},{4,5},{5,4},{6,7},{7,6},{8,9},{9,8},{10,11... | collective-permute-start | bytes 1572872 | tf_op jit(solution)/shard_map/ppermute | solution.py:368
  121.8 4.6 %collective-permute-start.5 = (bf16[128,16,128]{2,1,0:T(8,128)(2,1)S(1)}, bf16[128,16,128]{2,1,0:T(8,128)(2,1)S(1)}, u32[]{:S(2)}, u32[]{:S(2)}) collective-permute-start(bf16[128,16,128]{2,1,0:T(8,128)(2,1)S(1)} %collective-permute-done.1.refs_1_), channel_id=1, source_target_pairs={{0,1},{1,0},{2,3},{3,2},{4,5},{5,4},{6,7},{7,6},{8,9},{9,8},{10,11... | collective-permute-start | bytes 1572872 | tf_op jit(solution)/shard_map/ppermute | solution.py:368
  121.8 4.6 %collective-permute-start.6 = (bf16[128,16,128]{2,1,0:T(8,128)(2,1)S(1)}, bf16[128,16,128]{2,1,0:T(8,128)(2,1)S(1)}, u32[]{:S(2)}, u32[]{:S(2)}) collective-permute-start(bf16[128,16,128]{2,1,0:T(8,128)(2,1)S(1)} %collective-permute-done.2.refs_2_), channel_id=1, source_target_pairs={{0,1},{1,0},{2,3},{3,2},{4,5},{5,4},{6,7},{7,6},{8,9},{9,8},{10,11... | collective-permute-start | bytes 1572872 | tf_op jit(solution)/shard_map/ppermute | solution.py:368
